TPU v7x, 512 devices: a whole 4x8x8 slice. The times are simulated.
512 devices in a mesh: dp: 128 (over y, z, core), mp: 4 (over x).
Axes of the slice: x: 4, y: 8, z: 8, core: 2. Of those that a mesh axis runs over, the one named last changes fastest.
Arguments:
- query_hidden: bfloat16 [4096, 32, 768], P('dp', None, 'mp'), may hold values from -6 to 6
- query_proj: bfloat16 [768, 128], P('mp'), may hold values from -0.21875 to 0.21875
- passages: bfloat16 [8192, 128, 128], P(('dp', 'mp')), may hold values from -6 to 6
- teacher: float32 [4096, 4, 64], P('dp'), may hold values from -8 to 8
- neg_blocks: int32 [4096, 4], P('dp'), may hold values from 0 to 127, all different within a row; in each aligned block of 32 rows (0 to 31, 32 to 63, ...) at most 2 rows name the same one
Outputs:
- kl_loss: float32 [4096], P('dp')
Inputs may be any that keep to these rules, and one draw needn't show every extreme that they name: `neg_blocks`: each query names 4 different blocks. Among the 32 queries of one dp index no block is named more than 2 times, and some block is named exactly 2 times.
All inputs are finite; a program needn't handle non-finite values.
Results may differ from a plain program's by a relative error of at most 0.0003.
Values may be sent and summed in bfloat16 or wider, within the bound.
No kernel may reach another device: no remote copies, remote signals or barrier semaphores. Data moves between devices by JAX's collectives and lax.ppermute only.
A program may use at most 64 MiB of HBM per device.

v0:
```python
import jax
import jax.numpy as jnp
from jax import lax
from jax.sharding import PartitionSpec as P

softness = 0.1


def unit_rows(values):
    return values * lax.rsqrt(jnp.sum(values * values, axis=-1, keepdims=True) + 1e-06)


def soft_scores(slot_rows, passage_vecs):
    slot_count = slot_rows.shape[0]
    block_size = 16
    padded_count = -(-slot_count // block_size) * block_size
    blocked = slot_rows.reshape(
        padded_count // block_size, block_size, slot_rows.shape[1], slot_rows.shape[2]
    )

    def block_scores(slot_block):
        sims = jnp.einsum(
            "sie,pje->sipj", slot_block, passage_vecs, preferred_element_type=jnp.float32
        )
        softened = softness * jnp.log(jnp.sum(jnp.exp(sims / softness), axis=-1))
        return jnp.sum(softened, axis=1)

    scored = lax.map(block_scores, blocked)
    return scored.reshape(padded_count, -1)


def per_device(query_hidden, query_proj, passages, teacher, neg_blocks):
    partial_sum = jnp.einsum(
        "qth,he->qte", query_hidden, query_proj, preferred_element_type=jnp.float32
    )
    passage_vecs = unit_rows(passages.astype(jnp.float32)).astype(jnp.bfloat16)
    dp_count = lax.axis_size("dp")
    query_count, pick_count = neg_blocks.shape
    embed_width = partial_sum.shape[2]
    row_count = query_count * pick_count
    capacity = max(2, -(-row_count // dp_count))
    slots_all = dp_count * capacity
    owners = neg_blocks.reshape(row_count)
    owner_hits = (owners[:, None] == jnp.arange(dp_count, dtype=jnp.int32)[None, :]).astype(
        jnp.int32
    )
    earlier = jnp.cumsum(owner_hits, axis=0) - owner_hits
    slot_rank = jnp.sum(earlier * owner_hits, axis=1)
    slot_ids = owners * capacity + slot_rank
    matches = (slot_ids[None, :] == jnp.arange(slots_all, dtype=jnp.int32)[:, None]).astype(
        jnp.int32
    )
    row_query = jnp.arange(row_count, dtype=jnp.int32) // pick_count
    source = jnp.sum(matches * row_query[None, :], axis=1)
    filled = jnp.sum(matches, axis=1)
    projected = lax.psum(partial_sum, "mp")
    query_vecs = unit_rows(projected).astype(jnp.bfloat16)
    tokens = query_vecs.shape[1]
    outgoing = query_vecs[source] * filled[:, None, None].astype(jnp.bfloat16)
    outgoing = outgoing.reshape(dp_count, capacity, tokens, embed_width)
    arrived_items = lax.all_to_all(outgoing, "dp", split_axis=0, concat_axis=0, tiled=True)
    dims_items = arrived_items.shape
    flat_items = arrived_items.reshape(dims_items[0] * dims_items[1], dims_items[2], dims_items[3])
    scores = soft_scores(flat_items, passage_vecs).reshape(dims_items[0], dims_items[1], -1)
    returned = lax.all_to_all(scores, "dp", split_axis=0, concat_axis=0, tiled=True)
    home_scores = returned.reshape(slots_all, -1)[slot_ids].reshape(query_count, pick_count, -1)
    teacher_logp = teacher - jnp.log(jnp.sum(jnp.exp(teacher), axis=(1, 2), keepdims=True))
    student = lax.all_gather(home_scores, "mp", axis=2, tiled=True)
    kl_loss = jnp.sum(jnp.exp(teacher_logp) * (teacher_logp - student), axis=(1, 2)) + jnp.log(
        jnp.sum(jnp.exp(student), axis=(1, 2))
    )
    return kl_loss


def solution(mesh):
    in_specs = (
        P("dp", None, "mp"),
        P("mp", None),
        P(("dp", "mp"), None, None),
        P("dp", None, None),
        P("dp", None),
    )
    out_specs = P("dp")
    return jax.shard_map(
        per_device, mesh=mesh, in_specs=in_specs, out_specs=out_specs, check_vma=False
    )
```

profile of v0, /device:TPU:8, one launch (start us, length us, event | category | flops | bytes accessed | tf_op | source)
XLA Modules:
  0.0 229.7 jit_solution(16609151651576874862)
XLA Ops:
  6.5 1.0 copy-done
  7.6 1.9 fusion.7
  9.5 0.8 copy.19
  10.5 0.2 reduce_window_sum.11
  10.6 0.2 select_reduce_fusion.1
  10.8 0.2 convert_reduce_fusion
  11.0 0.2 convert_element_type.30
  11.2 57.0 %all-reduce.2.cloned.1.call-done = f32[32,32,128]{2,1,0:T(8,128)} async-done(((f32[32,32,128]{2,1,0:T(8,128)}), f32[32,32,128]{2,1,0:T(8,128)}) %all-reduce.2.cloned.1.call-update) | async-done | bytes 524304 | tf_op jit(solution)/shard_map/psum | solution.py:56
  68.2 1.2 multiply_reduce_fusion.1
  69.4 1.2 multiply_convert_fusion
  70.7 1.0 gather_fusion
  71.7 1.7 broadcast_multiply_fusion
  73.4 14.3 %all-to-all-start = ((bf16[128,2,32,128]{3,2,1,0:T(8,128)(2,1)}), bf16[128,2,32,128]{3,2,1,0:T(8,128)(2,1)S(1)}, u32[]{:S(2)}, u32[]{:S(2)}) async-start(bf16[128,2,32,128]{3,2,1,0:T(8,128)(2,1)} %broadcast_multiply_fusion), calls=%async_computation | async-start | bytes 4194304 | tf_op jit(solution)/shard_map/all_to_all | solution.py:61
  87.9 0.3 exponential_reduce_fusion.2
  88.2 0.3 fusion.4
  88.6 1.1 fusion.5
  89.8 50.3 %all-to-all-done = bf16[128,2,32,128]{3,2,1,0:T(8,128)(2,1)S(1)} async-done(((bf16[128,2,32,128]{3,2,1,0:T(8,128)(2,1)}), bf16[128,2,32,128]{3,2,1,0:T(8,128)(2,1)S(1)}, u32[]{:S(2)}, u32[]{:S(2)}) %all-to-all-start) | async-done | bytes 2097184 | tf_op jit(solution)/shard_map/all_to_all | solution.py:61
  140.1 49.7 %while.10 = (s32[]{:T(128)}, f32[16,16,16]{2,1,0:T(8,128)}, bf16[16,16,32,128]{3,2,1,0:T(8,128)(2,1)S(1)}, bf16[16,128,128]{2,1,0:T(8,128)(2,1)}, s32[]{:T(128)}) while((s32[]{:T(128)}, f32[16,16,16]{2,1,0:T(8,128)}, bf16[16,16,32,128]{3,2,1,0:T(8,128)(2,1)S(1)}, bf16[16,128,128]{2,1,0:T(8,128)(2,1)}, s32[]{:T(128)}) %tuple.25), condition=%wide.region_11.12_spmd, body=%wide.region_8.11_spmd.sunk | while | flops 270540544 | bytes 731713 | solution.py:28
  140.1 2.4 %exponential_reduce_fusion.4 = f32[16,32,16]{1,2,0:T(8,128)S(1)} fusion(bf16[16,128,128]{2,1,0:T(8,128)(2,1)} %get-tuple-element.78, bf16[16,16,32,128]{3,2,1,0:T(8,128)(2,1)S(1)} %get-tuple-element.77, s32[]{:T(128)} %get-tuple-element.70), kind=kOutput, calls=%fused_computation.2.clone.1 | convolution fusion | flops 270524416 | bytes 688132 | tf_op jit(solution)/shard_map/while/body/eval_jaxpr/sie,pje->sipj/dot_general | solution.py:22
  142.4 0.1 multiply_reduce_fusion.4
  142.6 0.6 bitcast_dynamic-update-slice_fusion.2
  143.2 2.4 %exponential_reduce_fusion.4 = f32[16,32,16]{1,2,0:T(8,128)S(1)} fusion(bf16[16,128,128]{2,1,0:T(8,128)(2,1)} %get-tuple-element.78, bf16[16,16,32,128]{3,2,1,0:T(8,128)(2,1)S(1)} %get-tuple-element.77, s32[]{:T(128)} %get-tuple-element.70), kind=kOutput, calls=%fused_computation.2.clone.1 | convolution fusion | flops 270524416 | bytes 688132 | tf_op jit(solution)/shard_map/while/body/eval_jaxpr/sie,pje->sipj/dot_general | solution.py:22
  145.5 0.1 multiply_reduce_fusion.4
  145.7 0.6 bitcast_dynamic-update-slice_fusion.2
  146.3 2.4 %exponential_reduce_fusion.4 = f32[16,32,16]{1,2,0:T(8,128)S(1)} fusion(bf16[16,128,128]{2,1,0:T(8,128)(2,1)} %get-tuple-element.78, bf16[16,16,32,128]{3,2,1,0:T(8,128)(2,1)S(1)} %get-tuple-element.77, s32[]{:T(128)} %get-tuple-element.70), kind=kOutput, calls=%fused_computation.2.clone.1 | convolution fusion | flops 270524416 | bytes 688132 | tf_op jit(solution)/shard_map/while/body/eval_jaxpr/sie,pje->sipj/dot_general | solution.py:22
  148.7 0.1 multiply_reduce_fusion.4
  148.8 0.6 bitcast_dynamic-update-slice_fusion.2
  149.4 2.4 %exponential_reduce_fusion.4 = f32[16,32,16]{1,2,0:T(8,128)S(1)} fusion(bf16[16,128,128]{2,1,0:T(8,128)(2,1)} %get-tuple-element.78, bf16[16,16,32,128]{3,2,1,0:T(8,128)(2,1)S(1)} %get-tuple-element.77, s32[]{:T(128)} %get-tuple-element.70), kind=kOutput, calls=%fused_computation.2.clone.1 | convolution fusion | flops 270524416 | bytes 688132 | tf_op jit(solution)/shard_map/while/body/eval_jaxpr/sie,pje->sipj/dot_general | solution.py:22
  151.8 0.1 multiply_reduce_fusion.4
  151.9 0.6 bitcast_dynamic-update-slice_fusion.2
  152.5 2.4 %exponential_reduce_fusion.4 = f32[16,32,16]{1,2,0:T(8,128)S(1)} fusion(bf16[16,128,128]{2,1,0:T(8,128)(2,1)} %get-tuple-element.78, bf16[16,16,32,128]{3,2,1,0:T(8,128)(2,1)S(1)} %get-tuple-element.77, s32[]{:T(128)} %get-tuple-element.70), kind=kOutput, calls=%fused_computation.2.clone.1 | convolution fusion | flops 270524416 | bytes 688132 | tf_op jit(solution)/shard_map/while/body/eval_jaxpr/sie,pje->sipj/dot_general | solution.py:22
  154.9 0.1 multiply_reduce_fusion.4
  155.0 0.6 bitcast_dynamic-update-slice_fusion.2
  155.6 2.4 %exponential_reduce_fusion.4 = f32[16,32,16]{1,2,0:T(8,128)S(1)} fusion(bf16[16,128,128]{2,1,0:T(8,128)(2,1)} %get-tuple-element.78, bf16[16,16,32,128]{3,2,1,0:T(8,128)(2,1)S(1)} %get-tuple-element.77, s32[]{:T(128)} %get-tuple-element.70), kind=kOutput, calls=%fused_computation.2.clone.1 | convolution fusion | flops 270524416 | bytes 688132 | tf_op jit(solution)/shard_map/while/body/eval_jaxpr/sie,pje->sipj/dot_general | solution.py:22
  158.0 0.1 multiply_reduce_fusion.4
  158.1 0.6 bitcast_dynamic-update-slice_fusion.2
  158.7 2.4 %exponential_reduce_fusion.4 = f32[16,32,16]{1,2,0:T(8,128)S(1)} fusion(bf16[16,128,128]{2,1,0:T(8,128)(2,1)} %get-tuple-element.78, bf16[16,16,32,128]{3,2,1,0:T(8,128)(2,1)S(1)} %get-tuple-element.77, s32[]{:T(128)} %get-tuple-element.70), kind=kOutput, calls=%fused_computation.2.clone.1 | convolution fusion | flops 270524416 | bytes 688132 | tf_op jit(solution)/shard_map/while/body/eval_jaxpr/sie,pje->sipj/dot_general | solution.py:22
  161.2 0.6 bitcast_dynamic-update-slice_fusion.2
  161.8 2.4 %exponential_reduce_fusion.4 = f32[16,32,16]{1,2,0:T(8,128)S(1)} fusion(bf16[16,128,128]{2,1,0:T(8,128)(2,1)} %get-tuple-element.78, bf16[16,16,32,128]{3,2,1,0:T(8,128)(2,1)S(1)} %get-tuple-element.77, s32[]{:T(128)} %get-tuple-element.70), kind=kOutput, calls=%fused_computation.2.clone.1 | convolution fusion | flops 270524416 | bytes 688132 | tf_op jit(solution)/shard_map/while/body/eval_jaxpr/sie,pje->sipj/dot_general | solution.py:22
  164.3 0.6 bitcast_dynamic-update-slice_fusion.2
  164.9 2.4 %exponential_reduce_fusion.4 = f32[16,32,16]{1,2,0:T(8,128)S(1)} fusion(bf16[16,128,128]{2,1,0:T(8,128)(2,1)} %get-tuple-element.78, bf16[16,16,32,128]{3,2,1,0:T(8,128)(2,1)S(1)} %get-tuple-element.77, s32[]{:T(128)} %get-tuple-element.70), kind=kOutput, calls=%fused_computation.2.clone.1 | convolution fusion | flops 270524416 | bytes 688132 | tf_op jit(solution)/shard_map/while/body/eval_jaxpr/sie,pje->sipj/dot_general | solution.py:22
  167.4 0.6 bitcast_dynamic-update-slice_fusion.2
  168.0 2.4 %exponential_reduce_fusion.4 = f32[16,32,16]{1,2,0:T(8,128)S(1)} fusion(bf16[16,128,128]{2,1,0:T(8,128)(2,1)} %get-tuple-element.78, bf16[16,16,32,128]{3,2,1,0:T(8,128)(2,1)S(1)} %get-tuple-element.77, s32[]{:T(128)} %get-tuple-element.70), kind=kOutput, calls=%fused_computation.2.clone.1 | convolution fusion | flops 270524416 | bytes 688132 | tf_op jit(solution)/shard_map/while/body/eval_jaxpr/sie,pje->sipj/dot_general | solution.py:22
  170.5 0.6 bitcast_dynamic-update-slice_fusion.2
  171.1 2.4 %exponential_reduce_fusion.4 = f32[16,32,16]{1,2,0:T(8,128)S(1)} fusion(bf16[16,128,128]{2,1,0:T(8,128)(2,1)} %get-tuple-element.78, bf16[16,16,32,128]{3,2,1,0:T(8,128)(2,1)S(1)} %get-tuple-element.77, s32[]{:T(128)} %get-tuple-element.70), kind=kOutput, calls=%fused_computation.2.clone.1 | convolution fusion | flops 270524416 | bytes 688132 | tf_op jit(solution)/shard_map/while/body/eval_jaxpr/sie,pje->sipj/dot_general | solution.py:22
  173.6 0.6 bitcast_dynamic-update-slice_fusion.2
  174.2 2.4 %exponential_reduce_fusion.4 = f32[16,32,16]{1,2,0:T(8,128)S(1)} fusion(bf16[16,128,128]{2,1,0:T(8,128)(2,1)} %get-tuple-element.78, bf16[16,16,32,128]{3,2,1,0:T(8,128)(2,1)S(1)} %get-tuple-element.77, s32[]{:T(128)} %get-tuple-element.70), kind=kOutput, calls=%fused_computation.2.clone.1 | convolution fusion | flops 270524416 | bytes 688132 | tf_op jit(solution)/shard_map/while/body/eval_jaxpr/sie,pje->sipj/dot_general | solution.py:22
  176.6 0.1 multiply_reduce_fusion.4
  176.8 0.6 bitcast_dynamic-update-slice_fusion.2
  177.4 2.4 %exponential_reduce_fusion.4 = f32[16,32,16]{1,2,0:T(8,128)S(1)} fusion(bf16[16,128,128]{2,1,0:T(8,128)(2,1)} %get-tuple-element.78, bf16[16,16,32,128]{3,2,1,0:T(8,128)(2,1)S(1)} %get-tuple-element.77, s32[]{:T(128)} %get-tuple-element.70), kind=kOutput, calls=%fused_computation.2.clone.1 | convolution fusion | flops 270524416 | bytes 688132 | tf_op jit(solution)/shard_map/while/body/eval_jaxpr/sie,pje->sipj/dot_general | solution.py:22
  179.9 0.6 bitcast_dynamic-update-slice_fusion.2
  180.5 2.4 %exponential_reduce_fusion.4 = f32[16,32,16]{1,2,0:T(8,128)S(1)} fusion(bf16[16,128,128]{2,1,0:T(8,128)(2,1)} %get-tuple-element.78, bf16[16,16,32,128]{3,2,1,0:T(8,128)(2,1)S(1)} %get-tuple-element.77, s32[]{:T(128)} %get-tuple-element.70), kind=kOutput, calls=%fused_computation.2.clone.1 | convolution fusion | flops 270524416 | bytes 688132 | tf_op jit(solution)/shard_map/while/body/eval_jaxpr/sie,pje->sipj/dot_general | solution.py:22
  182.9 0.1 multiply_reduce_fusion.4
  183.0 0.6 bitcast_dynamic-update-slice_fusion.2
  183.6 2.4 %exponential_reduce_fusion.4 = f32[16,32,16]{1,2,0:T(8,128)S(1)} fusion(bf16[16,128,128]{2,1,0:T(8,128)(2,1)} %get-tuple-element.78, bf16[16,16,32,128]{3,2,1,0:T(8,128)(2,1)S(1)} %get-tuple-element.77, s32[]{:T(128)} %get-tuple-element.70), kind=kOutput, calls=%fused_computation.2.clone.1 | convolution fusion | flops 270524416 | bytes 688132 | tf_op jit(solution)/shard_map/while/body/eval_jaxpr/sie,pje->sipj/dot_general | solution.py:22
  186.1 0.6 bitcast_dynamic-update-slice_fusion.2
  186.7 2.4 %exponential_reduce_fusion.4 = f32[16,32,16]{1,2,0:T(8,128)S(1)} fusion(bf16[16,128,128]{2,1,0:T(8,128)(2,1)} %get-tuple-element.78, bf16[16,16,32,128]{3,2,1,0:T(8,128)(2,1)S(1)} %get-tuple-element.77, s32[]{:T(128)} %get-tuple-element.70), kind=kOutput, calls=%fused_computation.2.clone.1 | convolution fusion | flops 270524416 | bytes 688132 | tf_op jit(solution)/shard_map/while/body/eval_jaxpr/sie,pje->sipj/dot_general | solution.py:22
  189.2 0.6 bitcast_dynamic-update-slice_fusion.2
  189.8 7.5 %all-to-all-start.1 = ((f32[128,2,16]{2,1,0:T(2,128)}), f32[128,2,16]{2,1,0:T(2,128)S(1)}, u32[]{:S(2)}, u32[]{:S(2)}) async-start(f32[128,2,16]{2,1,0:T(2,128)} %bitcast.10), calls=%async_computation.1 | async-start | bytes 262144 | tf_op jit(solution)/shard_map/all_to_all | solution.py:65
  197.3 11.9 %all-to-all-done.1 = f32[128,2,16]{2,1,0:T(2,128)S(1)} async-done(((f32[128,2,16]{2,1,0:T(2,128)}), f32[128,2,16]{2,1,0:T(2,128)S(1)}, u32[]{:S(2)}, u32[]{:S(2)}) %all-to-all-start.1) | async-done | bytes 16416 | tf_op jit(solution)/shard_map/all_to_all | solution.py:65
  209.2 0.6 gather_fusion.1
  209.9 12.0 %all_gather.3 = f32[32,4,64]{0,1,2:T(4,128)S(1)} all-gather(f32[32,4,16]{0,1,2:T(4,128)S(1)} %copy.21), channel_id=1, replica_groups=mesh['dp'=128,'mp'=4] {'mp'}, dimensions={2}, use_global_device_ids=true | all-gather | bytes 40960 | tf_op jit(solution)/shard_map/all_gather | solution.py:68
  222.1 0.2 multiply_reduce_fusion.2
  222.3 0.5 log_add_fusion
  (35 shorter events, 1.7 us)
Async XLA Ops:
  6.5 1.0 copy-start
  6.5 61.6 %all-reduce.2.cloned.1.call-start = ((), (), s32[]{:S(2)}) async-start(), calls=%async_computation.2 | async-start | bytes 1048576 | tf_op jit(solution)/shard_map/psum | solution.py:56
  73.4 14.3 %copy-start.3 = (s32[32,4]{0,1:T(4,128)S(1)}, s32[32,4]{0,1:T(4,128)}, u32[]{:S(2)}) copy-start(s32[32,4]{0,1:T(4,128)} %param.11) | copy-start | bytes 1540
  73.4 14.5 %copy-start.2 = (f32[32,4,64]{2,1,0:T(4,128)S(1)}, f32[32,4,64]{2,1,0:T(4,128)}, u32[]{:S(2)}) copy-start(f32[32,4,64]{2,1,0:T(4,128)} %param.10) | copy-start | bytes 98308
  73.4 14.9 %copy-start.1 = (bf16[16,128,128]{2,1,0:T(8,128)(2,1)S(1)}, bf16[16,128,128]{2,1,0:T(8,128)(2,1)}, u32[]{:S(2)}) copy-start(bf16[16,128,128]{2,1,0:T(8,128)(2,1)} %param.9) | copy-start | bytes 1572868
  73.4 66.7 %all-to-all-start = ((bf16[128,2,32,128]{3,2,1,0:T(8,128)(2,1)}), bf16[128,2,32,128]{3,2,1,0:T(8,128)(2,1)S(1)}, u32[]{:S(2)}, u32[]{:S(2)}) async-start(bf16[128,2,32,128]{3,2,1,0:T(8,128)(2,1)} %broadcast_multiply_fusion), calls=%async_computation | async-start | bytes 4194304 | tf_op jit(solution)/shard_map/all_to_all | solution.py:61
  189.8 19.4 %all-to-all-start.1 = ((f32[128,2,16]{2,1,0:T(2,128)}), f32[128,2,16]{2,1,0:T(2,128)S(1)}, u32[]{:S(2)}, u32[]{:S(2)}) async-start(f32[128,2,16]{2,1,0:T(2,128)} %bitcast.10), calls=%async_computation.1 | async-start | bytes 262144 | tf_op jit(solution)/shard_map/all_to_all | solution.py:65
Sparse Core Ops, SparseCore 0:
  9.7 58.4 all-reduce.1
where the time goes:
time: 231 us; the launch traced here: 230 us
  waiting for transfers between devices  119 us (52%)
  matrix products  39.9 us (17%)
  starting transfers between devices  21.8 us (9%)
  local copies, waits for them, and re-layouts  13.7 us (6%)
  between operations  13.6 us (6%)
  blocking collectives  12 us (5%)
  other arithmetic  9.3 us (4%)
    psum x1, waiting for transfers between devices, per_device(): projected = lax.psum(partial_sum, 'mp')  57 us
    all_to_all x1, waiting for transfers between devices, per_device(): lax.all_to_all(outgoing, 'dp', split_axis=0, concat_axis=0, tiled=True)  50.3 us
    dot_general x16, matrix products, block_scores(): jnp.einsum('sie,pje->sipj', slot_block, passage_vecs, preferred_element_t...  38 us
    all_to_all x1, starting transfers between devices, per_device(): lax.all_to_all(outgoing, 'dp', split_axis=0, concat_axis=0, tiled=True)  14.3 us
    all_gather x1, blocking collectives, per_device(): student = lax.all_gather(home_scores, 'mp', axis=2, tiled=True)  12 us
    all_to_all x1, waiting for transfers between devices, per_device(): lax.all_to_all(scores, 'dp', split_axis=0, concat_axis=0, tiled=True)  11.9 us
    dynamic_update_slice x16, local copies, waits for them, and re-layouts, soft_scores(): scored = lax.map(block_scores, blocked)  9.63 us
    all_to_all x1, starting transfers between devices, per_device(): lax.all_to_all(scores, 'dp', split_axis=0, concat_axis=0, tiled=True)  7.48 us
  transfers between devices with their start and end apart: 3, of which 3 were waited for; matrix products, arithmetic and copies ran while one was open for 2% of the time, Pallas kernels for 0%

commit v1 on v0

--- a/solution.py
+++ b/solution.py
@@ -53,7 +53,7 @@
     row_query = jnp.arange(row_count, dtype=jnp.int32) // pick_count
     source = jnp.sum(matches * row_query[None, :], axis=1)
     filled = jnp.sum(matches, axis=1)
-    projected = lax.psum(partial_sum, "mp")
+    projected = jnp.sum(lax.all_gather(partial_sum, axis_name="mp"), 0)
     query_vecs = unit_rows(projected).astype(jnp.bfloat16)
     tokens = query_vecs.shape[1]
     outgoing = query_vecs[source] * filled[:, None, None].astype(jnp.bfloat16)

time: 231 us -> 213 us (0.922)
  waiting for transfers between devices: 119 us -> 101 us
    psum x1 -> x0, waiting for transfers between devices: 57 us -> none  [per_device(): projected = lax.psum(partial_sum, 'mp')]
    all_gather x0 -> x1, waiting for transfers between devices: none -> 39.1 us  [per_device(): projected = jnp.sum(lax.all_gather(partial_sum, axis_name='mp'), 0)]
where the time goes in v1:
time: 213 us; the launch traced here: 212 us
  waiting for transfers between devices  101 us (47%)
  matrix products  39.9 us (19%)
  starting transfers between devices  21.8 us (10%)
  local copies, waits for them, and re-layouts  13.7 us (6%)
  between operations  13.6 us (6%)
  blocking collectives  12 us (6%)
  other arithmetic  9.09 us (4%)
    all_to_all x1, waiting for transfers between devices, per_device(): lax.all_to_all(outgoing, 'dp', split_axis=0, concat_axis=0, tiled=True)  50.3 us
    all_gather x1, waiting for transfers between devices, per_device(): projected = jnp.sum(lax.all_gather(partial_sum, axis_name='mp'), 0)  39.1 us
    dot_general x16, matrix products, block_scores(): jnp.einsum('sie,pje->sipj', slot_block, passage_vecs, preferred_element_t...  38 us
    all_to_all x1, starting transfers between devices, per_device(): lax.all_to_all(outgoing, 'dp', split_axis=0, concat_axis=0, tiled=True)  14.3 us
    all_gather x1, blocking collectives, per_device(): student = lax.all_gather(home_scores, 'mp', axis=2, tiled=True)  12 us
    all_to_all x1, waiting for transfers between devices, per_device(): lax.all_to_all(scores, 'dp', split_axis=0, concat_axis=0, tiled=True)  11.9 us
    dynamic_update_slice x16, local copies, waits for them, and re-layouts, soft_scores(): scored = lax.map(block_scores, blocked)  9.63 us
    all_to_all x1, starting transfers between devices, per_device(): lax.all_to_all(scores, 'dp', split_axis=0, concat_axis=0, tiled=True)  7.47 us
  transfers between devices with their start and end apart: 3, of which 3 were waited for; matrix products, arithmetic and copies ran while one was open for 2% of the time, Pallas kernels for 0%

profile of v1, /device:TPU:8, one launch (start us, length us, event | category | flops | bytes accessed | tf_op | source)
XLA Modules:
  0.0 211.6 jit_solution(6854126806094070366)
XLA Ops:
  6.5 1.0 copy-done
  7.6 1.9 fusion.7
  9.5 0.8 copy.19
  10.5 0.2 reduce_window_sum.11
  10.6 0.2 select_reduce_fusion.1
  10.8 0.2 convert_reduce_fusion
  11.0 0.2 convert_element_type.30
  11.2 39.1 %all-gather.3.cloned.1.call-done = f32[128,32,128]{2,1,0:T(8,128)} async-done(((f32[32,32,128]{2,1,0:T(8,128)}), f32[128,32,128]{2,1,0:T(8,128)}) %all-gather.3.cloned.1.call-update) | async-done | bytes 2097168 | tf_op jit(solution)/shard_map/all_gather | solution.py:56
  50.3 1.9 reduce_sum.104
  52.2 0.2 multiply_reduce_fusion.1
  52.4 0.2 multiply_convert_fusion
  52.6 1.0 gather_fusion
  53.6 1.7 broadcast_multiply_fusion
  55.3 14.3 %all-to-all-start = ((bf16[128,2,32,128]{3,2,1,0:T(8,128)(2,1)}), bf16[128,2,32,128]{3,2,1,0:T(8,128)(2,1)S(1)}, u32[]{:S(2)}, u32[]{:S(2)}) async-start(bf16[128,2,32,128]{3,2,1,0:T(8,128)(2,1)} %broadcast_multiply_fusion), calls=%async_computation | async-start | bytes 4194304 | tf_op jit(solution)/shard_map/all_to_all | solution.py:61
  69.8 0.3 exponential_reduce_fusion.2
  70.2 0.3 fusion.4
  70.6 1.1 fusion.5
  71.7 50.3 %all-to-all-done = bf16[128,2,32,128]{3,2,1,0:T(8,128)(2,1)S(1)} async-done(((bf16[128,2,32,128]{3,2,1,0:T(8,128)(2,1)}), bf16[128,2,32,128]{3,2,1,0:T(8,128)(2,1)S(1)}, u32[]{:S(2)}, u32[]{:S(2)}) %all-to-all-start) | async-done | bytes 2097184 | tf_op jit(solution)/shard_map/all_to_all | solution.py:61
  122.0 49.7 %while.10 = (s32[]{:T(128)}, f32[16,16,16]{2,1,0:T(8,128)}, bf16[16,16,32,128]{3,2,1,0:T(8,128)(2,1)S(1)}, bf16[16,128,128]{2,1,0:T(8,128)(2,1)}, s32[]{:T(128)}) while((s32[]{:T(128)}, f32[16,16,16]{2,1,0:T(8,128)}, bf16[16,16,32,128]{3,2,1,0:T(8,128)(2,1)S(1)}, bf16[16,128,128]{2,1,0:T(8,128)(2,1)}, s32[]{:T(128)}) %tuple.25), condition=%wide.region_11.12_spmd, body=%wide.region_8.11_spmd.sunk | while | flops 270540544 | bytes 731713 | solution.py:28
  122.0 2.4 %exponential_reduce_fusion.4 = f32[16,32,16]{1,2,0:T(8,128)S(1)} fusion(bf16[16,128,128]{2,1,0:T(8,128)(2,1)} %get-tuple-element.78, bf16[16,16,32,128]{3,2,1,0:T(8,128)(2,1)S(1)} %get-tuple-element.77, s32[]{:T(128)} %get-tuple-element.70), kind=kOutput, calls=%fused_computation.2.clone.1 | convolution fusion | flops 270524416 | bytes 688132 | tf_op jit(solution)/shard_map/while/body/eval_jaxpr/sie,pje->sipj/dot_general | solution.py:22
  124.4 0.1 multiply_reduce_fusion.4
  124.5 0.6 bitcast_dynamic-update-slice_fusion.2
  125.1 2.4 %exponential_reduce_fusion.4 = f32[16,32,16]{1,2,0:T(8,128)S(1)} fusion(bf16[16,128,128]{2,1,0:T(8,128)(2,1)} %get-tuple-element.78, bf16[16,16,32,128]{3,2,1,0:T(8,128)(2,1)S(1)} %get-tuple-element.77, s32[]{:T(128)} %get-tuple-element.70), kind=kOutput, calls=%fused_computation.2.clone.1 | convolution fusion | flops 270524416 | bytes 688132 | tf_op jit(solution)/shard_map/while/body/eval_jaxpr/sie,pje->sipj/dot_general | solution.py:22
  127.5 0.1 multiply_reduce_fusion.4
  127.6 0.6 bitcast_dynamic-update-slice_fusion.2
  128.2 2.4 %exponential_reduce_fusion.4 = f32[16,32,16]{1,2,0:T(8,128)S(1)} fusion(bf16[16,128,128]{2,1,0:T(8,128)(2,1)} %get-tuple-element.78, bf16[16,16,32,128]{3,2,1,0:T(8,128)(2,1)S(1)} %get-tuple-element.77, s32[]{:T(128)} %get-tuple-element.70), kind=kOutput, calls=%fused_computation.2.clone.1 | convolution fusion | flops 270524416 | bytes 688132 | tf_op jit(solution)/shard_map/while/body/eval_jaxpr/sie,pje->sipj/dot_general | solution.py:22
  130.6 0.1 multiply_reduce_fusion.4
  130.7 0.6 bitcast_dynamic-update-slice_fusion.2
  131.3 2.4 %exponential_reduce_fusion.4 = f32[16,32,16]{1,2,0:T(8,128)S(1)} fusion(bf16[16,128,128]{2,1,0:T(8,128)(2,1)} %get-tuple-element.78, bf16[16,16,32,128]{3,2,1,0:T(8,128)(2,1)S(1)} %get-tuple-element.77, s32[]{:T(128)} %get-tuple-element.70), kind=kOutput, calls=%fused_computation.2.clone.1 | convolution fusion | flops 270524416 | bytes 688132 | tf_op jit(solution)/shard_map/while/body/eval_jaxpr/sie,pje->sipj/dot_general | solution.py:22
  133.7 0.1 multiply_reduce_fusion.4
  133.8 0.6 bitcast_dynamic-update-slice_fusion.2
  134.4 2.4 %exponential_reduce_fusion.4 = f32[16,32,16]{1,2,0:T(8,128)S(1)} fusion(bf16[16,128,128]{2,1,0:T(8,128)(2,1)} %get-tuple-element.78, bf16[16,16,32,128]{3,2,1,0:T(8,128)(2,1)S(1)} %get-tuple-element.77, s32[]{:T(128)} %get-tuple-element.70), kind=kOutput, calls=%fused_computation.2.clone.1 | convolution fusion | flops 270524416 | bytes 688132 | tf_op jit(solution)/shard_map/while/body/eval_jaxpr/sie,pje->sipj/dot_general | solution.py:22
  136.8 0.1 multiply_reduce_fusion.4
  136.9 0.6 bitcast_dynamic-update-slice_fusion.2
  137.5 2.4 %exponential_reduce_fusion.4 = f32[16,32,16]{1,2,0:T(8,128)S(1)} fusion(bf16[16,128,128]{2,1,0:T(8,128)(2,1)} %get-tuple-element.78, bf16[16,16,32,128]{3,2,1,0:T(8,128)(2,1)S(1)} %get-tuple-element.77, s32[]{:T(128)} %get-tuple-element.70), kind=kOutput, calls=%fused_computation.2.clone.1 | convolution fusion | flops 270524416 | bytes 688132 | tf_op jit(solution)/shard_map/while/body/eval_jaxpr/sie,pje->sipj/dot_general | solution.py:22
  140.0 0.6 bitcast_dynamic-update-slice_fusion.2
  140.6 2.4 %exponential_reduce_fusion.4 = f32[16,32,16]{1,2,0:T(8,128)S(1)} fusion(bf16[16,128,128]{2,1,0:T(8,128)(2,1)} %get-tuple-element.78, bf16[16,16,32,128]{3,2,1,0:T(8,128)(2,1)S(1)} %get-tuple-element.77, s32[]{:T(128)} %get-tuple-element.70), kind=kOutput, calls=%fused_computation.2.clone.1 | convolution fusion | flops 270524416 | bytes 688132 | tf_op jit(solution)/shard_map/while/body/eval_jaxpr/sie,pje->sipj/dot_general | solution.py:22
  143.1 0.6 bitcast_dynamic-update-slice_fusion.2
  143.7 2.4 %exponential_reduce_fusion.4 = f32[16,32,16]{1,2,0:T(8,128)S(1)} fusion(bf16[16,128,128]{2,1,0:T(8,128)(2,1)} %get-tuple-element.78, bf16[16,16,32,128]{3,2,1,0:T(8,128)(2,1)S(1)} %get-tuple-element.77, s32[]{:T(128)} %get-tuple-element.70), kind=kOutput, calls=%fused_computation.2.clone.1 | convolution fusion | flops 270524416 | bytes 688132 | tf_op jit(solution)/shard_map/while/body/eval_jaxpr/sie,pje->sipj/dot_general | solution.py:22
  146.3 0.6 bitcast_dynamic-update-slice_fusion.2
  146.9 2.4 %exponential_reduce_fusion.4 = f32[16,32,16]{1,2,0:T(8,128)S(1)} fusion(bf16[16,128,128]{2,1,0:T(8,128)(2,1)} %get-tuple-element.78, bf16[16,16,32,128]{3,2,1,0:T(8,128)(2,1)S(1)} %get-tuple-element.77, s32[]{:T(128)} %get-tuple-element.70), kind=kOutput, calls=%fused_computation.2.clone.1 | convolution fusion | flops 270524416 | bytes 688132 | tf_op jit(solution)/shard_map/while/body/eval_jaxpr/sie,pje->sipj/dot_general | solution.py:22
  149.4 0.6 bitcast_dynamic-update-slice_fusion.2
  150.0 2.4 %exponential_reduce_fusion.4 = f32[16,32,16]{1,2,0:T(8,128)S(1)} fusion(bf16[16,128,128]{2,1,0:T(8,128)(2,1)} %get-tuple-element.78, bf16[16,16,32,128]{3,2,1,0:T(8,128)(2,1)S(1)} %get-tuple-element.77, s32[]{:T(128)} %get-tuple-element.70), kind=kOutput, calls=%fused_computation.2.clone.1 | convolution fusion | flops 270524416 | bytes 688132 | tf_op jit(solution)/shard_map/while/body/eval_jaxpr/sie,pje->sipj/dot_general | solution.py:22
  152.5 0.6 bitcast_dynamic-update-slice_fusion.2
  153.1 2.4 %exponential_reduce_fusion.4 = f32[16,32,16]{1,2,0:T(8,128)S(1)} fusion(bf16[16,128,128]{2,1,0:T(8,128)(2,1)} %get-tuple-element.78, bf16[16,16,32,128]{3,2,1,0:T(8,128)(2,1)S(1)} %get-tuple-element.77, s32[]{:T(128)} %get-tuple-element.70), kind=kOutput, calls=%fused_computation.2.clone.1 | convolution fusion | flops 270524416 | bytes 688132 | tf_op jit(solution)/shard_map/while/body/eval_jaxpr/sie,pje->sipj/dot_general | solution.py:22
  155.6 0.6 bitcast_dynamic-update-slice_fusion.2
  156.2 2.4 %exponential_reduce_fusion.4 = f32[16,32,16]{1,2,0:T(8,128)S(1)} fusion(bf16[16,128,128]{2,1,0:T(8,128)(2,1)} %get-tuple-element.78, bf16[16,16,32,128]{3,2,1,0:T(8,128)(2,1)S(1)} %get-tuple-element.77, s32[]{:T(128)} %get-tuple-element.70), kind=kOutput, calls=%fused_computation.2.clone.1 | convolution fusion | flops 270524416 | bytes 688132 | tf_op jit(solution)/shard_map/while/body/eval_jaxpr/sie,pje->sipj/dot_general | solution.py:22
  158.7 0.6 bitcast_dynamic-update-slice_fusion.2
  159.3 2.4 %exponential_reduce_fusion.4 = f32[16,32,16]{1,2,0:T(8,128)S(1)} fusion(bf16[16,128,128]{2,1,0:T(8,128)(2,1)} %get-tuple-element.78, bf16[16,16,32,128]{3,2,1,0:T(8,128)(2,1)S(1)} %get-tuple-element.77, s32[]{:T(128)} %get-tuple-element.70), kind=kOutput, calls=%fused_computation.2.clone.1 | convolution fusion | flops 270524416 | bytes 688132 | tf_op jit(solution)/shard_map/while/body/eval_jaxpr/sie,pje->sipj/dot_general | solution.py:22
  161.7 0.1 multiply_reduce_fusion.4
  161.8 0.6 bitcast_dynamic-update-slice_fusion.2
  162.4 2.4 %exponential_reduce_fusion.4 = f32[16,32,16]{1,2,0:T(8,128)S(1)} fusion(bf16[16,128,128]{2,1,0:T(8,128)(2,1)} %get-tuple-element.78, bf16[16,16,32,128]{3,2,1,0:T(8,128)(2,1)S(1)} %get-tuple-element.77, s32[]{:T(128)} %get-tuple-element.70), kind=kOutput, calls=%fused_computation.2.clone.1 | convolution fusion | flops 270524416 | bytes 688132 | tf_op jit(solution)/shard_map/while/body/eval_jaxpr/sie,pje->sipj/dot_general | solution.py:22
  164.8 0.1 multiply_reduce_fusion.4
  164.9 0.6 bitcast_dynamic-update-slice_fusion.2
  165.5 2.4 %exponential_reduce_fusion.4 = f32[16,32,16]{1,2,0:T(8,128)S(1)} fusion(bf16[16,128,128]{2,1,0:T(8,128)(2,1)} %get-tuple-element.78, bf16[16,16,32,128]{3,2,1,0:T(8,128)(2,1)S(1)} %get-tuple-element.77, s32[]{:T(128)} %get-tuple-element.70), kind=kOutput, calls=%fused_computation.2.clone.1 | convolution fusion | flops 270524416 | bytes 688132 | tf_op jit(solution)/shard_map/while/body/eval_jaxpr/sie,pje->sipj/dot_general | solution.py:22
  168.0 0.6 bitcast_dynamic-update-slice_fusion.2
  168.6 2.4 %exponential_reduce_fusion.4 = f32[16,32,16]{1,2,0:T(8,128)S(1)} fusion(bf16[16,128,128]{2,1,0:T(8,128)(2,1)} %get-tuple-element.78, bf16[16,16,32,128]{3,2,1,0:T(8,128)(2,1)S(1)} %get-tuple-element.77, s32[]{:T(128)} %get-tuple-element.70), kind=kOutput, calls=%fused_computation.2.clone.1 | convolution fusion | flops 270524416 | bytes 688132 | tf_op jit(solution)/shard_map/while/body/eval_jaxpr/sie,pje->sipj/dot_general | solution.py:22
  171.1 0.6 bitcast_dynamic-update-slice_fusion.2
  171.7 7.5 %all-to-all-start.1 = ((f32[128,2,16]{2,1,0:T(2,128)}), f32[128,2,16]{2,1,0:T(2,128)S(1)}, u32[]{:S(2)}, u32[]{:S(2)}) async-start(f32[128,2,16]{2,1,0:T(2,128)} %bitcast.11), calls=%async_computation.1 | async-start | bytes 262144 | tf_op jit(solution)/shard_map/all_to_all | solution.py:65
  179.2 11.9 %all-to-all-done.1 = f32[128,2,16]{2,1,0:T(2,128)S(1)} async-done(((f32[128,2,16]{2,1,0:T(2,128)}), f32[128,2,16]{2,1,0:T(2,128)S(1)}, u32[]{:S(2)}, u32[]{:S(2)}) %all-to-all-start.1) | async-done | bytes 16416 | tf_op jit(solution)/shard_map/all_to_all | solution.py:65
  191.1 0.6 gather_fusion.1
  191.9 12.0 %all_gather.11 = f32[32,4,64]{0,1,2:T(4,128)S(1)} all-gather(f32[32,4,16]{0,1,2:T(4,128)S(1)} %copy.21), channel_id=1, replica_groups=mesh['dp'=128,'mp'=4] {'mp'}, dimensions={2}, use_global_device_ids=true | all-gather | bytes 40960 | tf_op jit(solution)/shard_map/all_gather | solution.py:68
  204.0 0.2 multiply_reduce_fusion.2
  204.2 0.5 log_add_fusion
  (36 shorter events, 1.8 us)
Async XLA Ops:
  6.5 1.0 copy-start
  6.5 43.8 %all-gather.3.cloned.1.call-start = ((), (), s32[]{:S(2)}) async-start(), calls=%async_computation.2 | async-start | bytes 2621440 | tf_op jit(solution)/shard_map/all_gather | solution.py:56
  55.3 14.3 %copy-start.3 = (s32[32,4]{0,1:T(4,128)S(1)}, s32[32,4]{0,1:T(4,128)}, u32[]{:S(2)}) copy-start(s32[32,4]{0,1:T(4,128)} %param.11) | copy-start | bytes 1540
  55.3 14.5 %copy-start.2 = (f32[32,4,64]{2,1,0:T(4,128)S(1)}, f32[32,4,64]{2,1,0:T(4,128)}, u32[]{:S(2)}) copy-start(f32[32,4,64]{2,1,0:T(4,128)} %param.10) | copy-start | bytes 98308
  55.3 14.9 %copy-start.1 = (bf16[16,128,128]{2,1,0:T(8,128)(2,1)S(1)}, bf16[16,128,128]{2,1,0:T(8,128)(2,1)}, u32[]{:S(2)}) copy-start(bf16[16,128,128]{2,1,0:T(8,128)(2,1)} %param.9) | copy-start | bytes 1572868
  55.3 66.7 %all-to-all-start = ((bf16[128,2,32,128]{3,2,1,0:T(8,128)(2,1)}), bf16[128,2,32,128]{3,2,1,0:T(8,128)(2,1)S(1)}, u32[]{:S(2)}, u32[]{:S(2)}) async-start(bf16[128,2,32,128]{3,2,1,0:T(8,128)(2,1)} %broadcast_multiply_fusion), calls=%async_computation | async-start | bytes 4194304 | tf_op jit(solution)/shard_map/all_to_all | solution.py:61
  171.7 19.4 %all-to-all-start.1 = ((f32[128,2,16]{2,1,0:T(2,128)}), f32[128,2,16]{2,1,0:T(2,128)S(1)}, u32[]{:S(2)}, u32[]{:S(2)}) async-start(f32[128,2,16]{2,1,0:T(2,128)} %bitcast.11), calls=%async_computation.1 | async-start | bytes 262144 | tf_op jit(solution)/shard_map/all_to_all | solution.py:65
Sparse Core Ops, SparseCore 0:
  9.6 40.6 all-gather.2
